TPU v7x, 32 devices: a whole 2x2x4 slice. The times are simulated.
32 devices in a mesh: dp: 8 (over z, core), expert: 4 (over y, x).
Axes of the slice: x: 2, y: 2, z: 4, core: 2. Of those that a mesh axis runs over, the one named last changes fastest.
Arguments:
- embedded: bfloat16 [64, 197, 512], P(('dp', 'expert')), may hold values from -6 to 6
- cotangent: bfloat16 [64, 197, 512], P(('dp', 'expert')), may hold values from -6 to 6
- w_qkv: bfloat16 [2, 512, 1536], P(None, 'dp'), may hold values from -0.25 to 0.25
- w_proj: bfloat16 [2, 512, 512], P(None, 'dp'), may hold values from -2.5 to 2.5
- w_router: bfloat16 [2, 512, 8], P(None, 'dp'), may hold values from -0.1875 to 0.1875
- norm_gains: bfloat16 [2, 2, 512], P(None, None, 'dp'), may hold values from 0.25 to 1.75
- norm_shifts: bfloat16 [2, 2, 512], P(None, None, 'dp'), may hold values from -1 to 1
- w_first: bfloat16 [2, 8, 512, 2048], P(None, 'expert', None, 'dp'), may hold values from -0.25 to 0.25
- w_second: bfloat16 [2, 8, 2048, 512], P(None, 'expert', 'dp'), may hold values from -1 to 1
- routes: int32 [2, 64, 197, 2], P(None, ('dp', 'expert')), may hold values from 0 to 7, all different within a row; in each aligned block of 394 rows (0 to 393, 394 to 787, ..., all dimensions but the last counted through in order) at most 147 rows name the same one
Outputs:
- out_images: bfloat16 [64, 197, 512], P(('dp', 'expert'))
- grad_images: float32 [64, 197, 512], P(('dp', 'expert'))
- grad_qkv: float32 [2, 512, 1536], P(None, 'dp')
- grad_proj: float32 [2, 512, 512], P(None, 'dp')
- grad_router: float32 [2, 512, 8], P(None, 'dp')
- grad_gains: float32 [2, 2, 512], P(None, None, 'dp')
- grad_shifts: float32 [2, 2, 512], P(None, None, 'dp')
- grad_first: float32 [2, 8, 512, 2048], P(None, 'expert', None, 'dp')
- grad_second: float32 [2, 8, 2048, 512], P(None, 'expert', 'dp')
Inputs may be any that keep to these rules, and one draw needn't show every extreme that they name: `routes`: the two experts of a token differ. Among the 394 tokens of one device in one block, no expert is named by more than 147 tokens, a bound that some block reaches.
All inputs are finite; a program needn't handle non-finite values.
Results may differ from a plain program's by a relative error of at most 0.019.
Values may be sent and summed in bfloat16 or wider, within the bound.
No kernel may reach another device: no remote copies, remote signals or barrier semaphores. Data moves between devices by JAX's collectives and lax.ppermute only.
A program may use at most 192 MiB of HBM per device.

v0:
```python
import jax
import jax.numpy as jnp
from jax import lax
from jax.sharding import PartitionSpec as P

HEADS = 8
HEAD_DIM = 64
SEQ = 197
LAYERS = 2
EPSILON = 1e-06
ROOT_HALF = 0.7071067811865476
INV_ROOT_TAU = 0.3989422804014327


def layer_norm(values, scale_in, shift_in):
    center = values - jnp.mean(values, axis=-1, keepdims=True)
    variance = jnp.mean(center * center, axis=-1, keepdims=True)
    inverse = lax.rsqrt(variance + EPSILON)
    normed = center * inverse
    return (normed * scale_in + shift_in, normed, inverse)


def norm_back(grad_out, normed, inverse, scale_in):
    grad_normed = grad_out * scale_in
    first_mean = jnp.mean(grad_normed, axis=-1, keepdims=True)
    second_mean = jnp.mean(grad_normed * normed, axis=-1, keepdims=True)
    grad_in = inverse * (grad_normed - first_mean - normed * second_mean)
    return (grad_in, jnp.sum(grad_out * normed, axis=0), jnp.sum(grad_out, axis=0))


def softmax_rows(scores):
    highest = jnp.max(scores, axis=-1, keepdims=True)
    powers = jnp.exp(scores - highest)
    row_total = jnp.sum(powers, axis=-1, keepdims=True)
    return (powers / row_total, highest + jnp.log(row_total))


def gelu_value(preact):
    return 0.5 * preact * (1.0 + lax.erf(preact * ROOT_HALF))


def gelu_slope(preact):
    return (
        0.5 * (1.0 + lax.erf(preact * ROOT_HALF))
        + preact * jnp.exp(-0.5 * preact * preact) * INV_ROOT_TAU
    )


def layer_forward(
    resid, which, w_qkv, w_proj, w_router, norm_gains, norm_shifts, w_first, w_second, routes
):
    qkv_full, proj_full, router_full, gains_full, shifts_full = (
        lax.all_gather(w_qkv[which], "dp", axis=0, tiled=True),
        lax.all_gather(w_proj[which], "dp", axis=0, tiled=True),
        lax.all_gather(w_router[which], "dp", axis=0, tiled=True),
        lax.all_gather(norm_gains[which], "dp", axis=1, tiled=True),
        lax.all_gather(norm_shifts[which], "dp", axis=1, tiled=True),
    )
    first_full, second_full = (
        lax.all_gather(w_first[which], "dp", axis=2, tiled=True),
        lax.all_gather(w_second[which], "dp", axis=1, tiled=True),
    )
    tok_count, width = resid.shape
    images = tok_count // SEQ
    gains_wide = gains_full.astype(jnp.float32)
    shifts_wide = shifts_full.astype(jnp.float32)
    attn_norm, unit_a, inv_a = layer_norm(resid, gains_wide[0], shifts_wide[0])
    attn_in = attn_norm.astype(jnp.bfloat16)
    packed = jnp.dot(attn_in, qkv_full, preferred_element_type=jnp.float32)
    head_shape = (images, SEQ, HEADS, HEAD_DIM)
    query = (packed[:, :width] * HEAD_DIM ** (-0.5)).astype(jnp.bfloat16).reshape(head_shape)
    keyed = packed[:, width : 2 * width].astype(jnp.bfloat16).reshape(head_shape)
    valued = packed[:, 2 * width :].astype(jnp.bfloat16).reshape(head_shape)
    scores = jnp.einsum("iqhd,ikhd->ihqk", query, keyed, preferred_element_type=jnp.float32)
    probs, log_total = softmax_rows(scores)
    mixed = jnp.einsum(
        "ihqk,ikhd->iqhd", probs.astype(jnp.bfloat16), valued, preferred_element_type=jnp.float32
    )
    mixed = mixed.reshape(tok_count, width).astype(jnp.bfloat16)
    resid_mid = resid + jnp.dot(mixed, proj_full, preferred_element_type=jnp.float32)
    moe_norm, unit_b, inv_b = layer_norm(resid_mid, gains_wide[1], shifts_wide[1])
    moe_in = moe_norm.astype(jnp.bfloat16)
    logits = jnp.dot(moe_in, router_full, preferred_element_type=jnp.float32)
    router_probs, ignored_total = softmax_rows(logits)
    experts_total = router_full.shape[1]
    local_count = first_full.shape[0]
    peers = lax.axis_size("expert")
    capacity = max(2, 3 * tok_count // experts_total)
    route = routes[which].reshape(tok_count, 2)
    labels = jnp.arange(experts_total, dtype=jnp.int32)
    pick_first = (route[:, 0:1] == labels[None, :]).astype(jnp.int32)
    pick_second = (route[:, 1:2] == labels[None, :]).astype(jnp.int32)
    both_picks = pick_first + pick_second
    before = jnp.cumsum(both_picks, axis=0) - both_picks
    slot_first = route[:, 0] * capacity + jnp.sum(before * pick_first, axis=1)
    slot_second = route[:, 1] * capacity + jnp.sum(before * pick_second, axis=1)
    slot_ids = jnp.arange(experts_total * capacity, dtype=jnp.int32)
    place_first = (slot_ids[:, None] == slot_first[None, :]).astype(jnp.bfloat16)
    place_second = (slot_ids[:, None] == slot_second[None, :]).astype(jnp.bfloat16)
    outgoing = jnp.dot(place_first + place_second, moe_in, preferred_element_type=jnp.float32)
    outgoing = outgoing.astype(jnp.bfloat16).reshape(peers, local_count, capacity, width)
    incoming = lax.all_to_all(outgoing, "expert", split_axis=0, concat_axis=0, tiled=True)
    hidden_pre = jnp.einsum(
        "sjcd,jdf->sjcf", incoming, first_full, preferred_element_type=jnp.float32
    )
    hidden_act = gelu_value(hidden_pre).astype(jnp.bfloat16)
    result = jnp.einsum(
        "sjcf,jfd->sjcd", hidden_act, second_full, preferred_element_type=jnp.float32
    ).astype(jnp.bfloat16)
    returned = lax.all_to_all(result, "expert", split_axis=0, concat_axis=0, tiled=True).reshape(
        experts_total * capacity, width
    )
    pick_first_f = pick_first.astype(jnp.float32)
    pick_second_f = pick_second.astype(jnp.float32)
    gate_first = jnp.sum(router_probs * pick_first_f, axis=1)
    gate_second = jnp.sum(router_probs * pick_second_f, axis=1)
    back_first = jnp.take(returned, slot_first, axis=0).astype(jnp.float32)
    back_second = jnp.take(returned, slot_second, axis=0).astype(jnp.float32)
    resid_out = resid_mid + (gate_first[:, None] * back_first + gate_second[:, None] * back_second)
    saved = (
        qkv_full,
        proj_full,
        router_full,
        gains_wide,
        first_full,
        second_full,
        unit_a,
        inv_a,
        attn_in,
        query,
        keyed,
        valued,
        log_total,
        mixed,
        unit_b,
        inv_b,
        moe_in,
        router_probs,
        pick_first_f,
        pick_second_f,
        slot_first,
        slot_second,
        place_first,
        place_second,
        incoming,
        hidden_pre,
        hidden_act,
        returned,
        gate_first,
        gate_second,
    )
    return (resid_out, saved)


def layer_backward(grad_out, saved):
    (
        qkv_full,
        proj_full,
        router_full,
        gains_wide,
        first_full,
        second_full,
        unit_a,
        inv_a,
        attn_in,
        query,
        keyed,
        valued,
        log_total,
        mixed,
        unit_b,
        inv_b,
        moe_in,
        router_probs,
        pick_first_f,
        pick_second_f,
        slot_first,
        slot_second,
        place_first,
        place_second,
        incoming,
        hidden_pre,
        hidden_act,
        returned,
        gate_first,
        gate_second,
    ) = saved
    tok_count, width = grad_out.shape
    images = tok_count // SEQ
    back_first = jnp.take(returned, slot_first, axis=0).astype(jnp.float32)
    back_second = jnp.take(returned, slot_second, axis=0).astype(jnp.float32)
    grad_gate_first = jnp.sum(grad_out * back_first, axis=1)
    grad_gate_second = jnp.sum(grad_out * back_second, axis=1)
    send_first = (gate_first[:, None] * grad_out).astype(jnp.bfloat16)
    send_second = (gate_second[:, None] * grad_out).astype(jnp.bfloat16)
    slot_grads = jnp.dot(place_first, send_first, preferred_element_type=jnp.float32) + jnp.dot(
        place_second, send_second, preferred_element_type=jnp.float32
    )
    slot_grads = slot_grads.astype(jnp.bfloat16).reshape(incoming.shape)
    grad_result = lax.all_to_all(slot_grads, "expert", split_axis=0, concat_axis=0, tiled=True)
    grad_act = jnp.einsum(
        "sjcd,jfd->sjcf", grad_result, second_full, preferred_element_type=jnp.float32
    )
    grad_second = jnp.einsum(
        "sjcf,sjcd->jfd", hidden_act, grad_result, preferred_element_type=jnp.float32
    )
    grad_pre = (grad_act * gelu_slope(hidden_pre)).astype(jnp.bfloat16)
    grad_first = jnp.einsum(
        "sjcd,sjcf->jdf", incoming, grad_pre, preferred_element_type=jnp.float32
    )
    grad_rows = jnp.einsum(
        "sjcf,jdf->sjcd", grad_pre, first_full, preferred_element_type=jnp.float32
    ).astype(jnp.bfloat16)
    grad_back = lax.all_to_all(
        grad_rows, "expert", split_axis=0, concat_axis=0, tiled=True
    ).reshape(-1, width)
    grad_moe = jnp.einsum(
        "st,sd->td", place_first + place_second, grad_back, preferred_element_type=jnp.float32
    )
    grad_probs = pick_first_f * grad_gate_first[:, None] + pick_second_f * grad_gate_second[:, None]
    weighted = jnp.sum(router_probs * grad_probs, axis=1, keepdims=True)
    grad_logits = (router_probs * (grad_probs - weighted)).astype(jnp.bfloat16)
    grad_router = jnp.einsum("td,te->de", moe_in, grad_logits, preferred_element_type=jnp.float32)
    grad_moe = grad_moe + jnp.einsum(
        "te,de->td", grad_logits, router_full, preferred_element_type=jnp.float32
    )
    grad_norm_b, gain_b_grad, shift_b_grad = norm_back(grad_moe, unit_b, inv_b, gains_wide[1])
    grad_mid = grad_out + grad_norm_b
    grad_branch = grad_mid.astype(jnp.bfloat16)
    grad_proj = jnp.einsum("td,te->de", mixed, grad_branch, preferred_element_type=jnp.float32)
    grad_mixed = jnp.einsum("te,de->td", grad_branch, proj_full, preferred_element_type=jnp.float32)
    grad_mixed = grad_mixed.astype(jnp.bfloat16).reshape(images, SEQ, HEADS, HEAD_DIM)
    scores = jnp.einsum("iqhd,ikhd->ihqk", query, keyed, preferred_element_type=jnp.float32)
    probs = jnp.exp(scores - log_total)
    grad_weights = jnp.einsum(
        "iqhd,ikhd->ihqk", grad_mixed, valued, preferred_element_type=jnp.float32
    )
    grad_valued = jnp.einsum(
        "ihqk,iqhd->ikhd",
        probs.astype(jnp.bfloat16),
        grad_mixed,
        preferred_element_type=jnp.float32,
    ).astype(jnp.bfloat16)
    row_inner = jnp.sum(probs * grad_weights, axis=-1, keepdims=True)
    grad_scores = (probs * (grad_weights - row_inner)).astype(jnp.bfloat16)
    grad_query = jnp.einsum(
        "ihqk,ikhd->iqhd", grad_scores, keyed, preferred_element_type=jnp.float32
    ).astype(jnp.bfloat16)
    grad_query = grad_query * jnp.asarray(HEAD_DIM ** (-0.5), jnp.bfloat16)
    grad_keyed = jnp.einsum(
        "ihqk,iqhd->ikhd", grad_scores, query, preferred_element_type=jnp.float32
    ).astype(jnp.bfloat16)
    grad_packed = jnp.concatenate(
        [
            grad_query.reshape(tok_count, width),
            grad_keyed.reshape(tok_count, width),
            grad_valued.reshape(tok_count, width),
        ],
        axis=1,
    )
    grad_qkv = jnp.einsum("td,te->de", attn_in, grad_packed, preferred_element_type=jnp.float32)
    grad_attn = jnp.einsum("te,de->td", grad_packed, qkv_full, preferred_element_type=jnp.float32)
    grad_norm_a, gain_a_grad, shift_a_grad = norm_back(grad_attn, unit_a, inv_a, gains_wide[0])
    grad_in = grad_mid + grad_norm_a
    dense = (
        grad_qkv,
        grad_proj,
        grad_router,
        jnp.stack([gain_a_grad, gain_b_grad]),
        jnp.stack([shift_a_grad, shift_b_grad]),
    )
    return (grad_in, dense, (grad_first, grad_second))


def body(
    embedded, cotangent, w_qkv, w_proj, w_router, norm_gains, norm_shifts, w_first, w_second, routes
):
    images, length, width = embedded.shape
    tok_count = images * length
    resid = embedded.reshape(tok_count, width).astype(jnp.float32)
    layer_inputs = []
    for which in range(LAYERS):
        layer_inputs.append(resid)
        resid, saved = layer_forward(
            resid,
            which,
            w_qkv,
            w_proj,
            w_router,
            norm_gains,
            norm_shifts,
            w_first,
            w_second,
            routes,
        )
    out_images = resid.reshape(images, length, width).astype(jnp.bfloat16)
    grad = cotangent.reshape(tok_count, width).astype(jnp.float32)
    dense_layers = []
    expert_layers = []
    for which in reversed(range(LAYERS)):
        ignored, saved = layer_forward(
            layer_inputs[which],
            which,
            w_qkv,
            w_proj,
            w_router,
            norm_gains,
            norm_shifts,
            w_first,
            w_second,
            routes,
        )
        grad, dense, expert_part = layer_backward(grad, saved)
        totals = (
            lax.psum(dense[0].astype(jnp.bfloat16), "expert").astype(jnp.float32),
            lax.psum(dense[1].astype(jnp.bfloat16), "expert").astype(jnp.float32),
            lax.psum(dense[2].astype(jnp.bfloat16), "expert").astype(jnp.float32),
            lax.psum(dense[3].astype(jnp.bfloat16), "expert").astype(jnp.float32),
            lax.psum(dense[4].astype(jnp.bfloat16), "expert").astype(jnp.float32),
        )
        shares = (
            lax.psum_scatter(
                totals[0].astype(jnp.bfloat16), "dp", scatter_dimension=0, tiled=True
            ).astype(jnp.float32),
            lax.psum_scatter(
                totals[1].astype(jnp.bfloat16), "dp", scatter_dimension=0, tiled=True
            ).astype(jnp.float32),
            lax.psum_scatter(
                totals[2].astype(jnp.bfloat16), "dp", scatter_dimension=0, tiled=True
            ).astype(jnp.float32),
            lax.psum_scatter(
                totals[3].astype(jnp.bfloat16), "dp", scatter_dimension=1, tiled=True
            ).astype(jnp.float32),
            lax.psum_scatter(
                totals[4].astype(jnp.bfloat16), "dp", scatter_dimension=1, tiled=True
            ).astype(jnp.float32),
        )
        expert_shares = (
            lax.psum_scatter(
                expert_part[0].astype(jnp.bfloat16), "dp", scatter_dimension=2, tiled=True
            ).astype(jnp.float32),
            lax.psum_scatter(
                expert_part[1].astype(jnp.bfloat16), "dp", scatter_dimension=1, tiled=True
            ).astype(jnp.float32),
        )
        dense_layers.insert(0, shares)
        expert_layers.insert(0, expert_shares)
    grad_images = grad.reshape(images, length, width)
    grad_qkv = jnp.stack([entry[0] for entry in dense_layers])
    grad_proj = jnp.stack([entry[1] for entry in dense_layers])
    grad_router = jnp.stack([entry[2] for entry in dense_layers])
    grad_gains = jnp.stack([entry[3] for entry in dense_layers])
    grad_shifts = jnp.stack([entry[4] for entry in dense_layers])
    grad_first = jnp.stack([entry[0] for entry in expert_layers])
    grad_second = jnp.stack([entry[1] for entry in expert_layers])
    return (
        out_images,
        grad_images,
        grad_qkv,
        grad_proj,
        grad_router,
        grad_gains,
        grad_shifts,
        grad_first,
        grad_second,
    )


def solution(mesh):
    return jax.shard_map(
        body,
        mesh=mesh,
        in_specs=(
            P(("dp", "expert"), None, None),
            P(("dp", "expert"), None, None),
            P(None, "dp", None),
            P(None, "dp", None),
            P(None, "dp", None),
            P(None, None, "dp"),
            P(None, None, "dp"),
            P(None, "expert", None, "dp"),
            P(None, "expert", "dp", None),
            P(None, ("dp", "expert"), None, None),
        ),
        out_specs=(
            P(("dp", "expert"), None, None),
            P(("dp", "expert"), None, None),
            P(None, "dp", None),
            P(None, "dp", None),
            P(None, "dp", None),
            P(None, None, "dp"),
            P(None, None, "dp"),
            P(None, "expert", None, "dp"),
            P(None, "expert", "dp", None),
        ),
        check_vma=False,
    )
```

profile of v0, /device:TPU:0, one launch (start us, length us, event | category | flops | bytes accessed | tf_op | source)
XLA Modules:
  0.0 1092.9 jit_solution(856967177096205174)
XLA Ops:
  16.5 17.0 %all-gather = bf16[1,2,512]{1,0,2:T(2,128)(2,1)S(1)} all-gather(bf16[1,2,64]{1,0,2:T(2,128)(2,1)S(1)} %copy.377), channel_id=2, replica_groups=mesh['dp'=8,'expert'=4] {'dp'}, dimensions={2}, use_global_device_ids=true | all-gather | bytes 2304 | tf_op jit(solution)/shard_map/all_gather | solution.py:56
  37.7 14.6 %all-gather.1 = bf16[1,2,512]{1,0,2:T(2,128)(2,1)S(1)} all-gather(bf16[1,2,64]{1,0,2:T(2,128)(2,1)S(1)} %copy.378), channel_id=3, replica_groups=mesh['dp'=8,'expert'=4] {'dp'}, dimensions={2}, use_global_device_ids=true | all-gather | bytes 2304 | tf_op jit(solution)/shard_map/all_gather | solution.py:57
  55.9 25.2 %all-gather.3 = bf16[1,512,512]{2,1,0:T(8,128)(2,1)} all-gather(bf16[1,64,512]{2,1,0:T(8,128)(2,1)S(1)} %get-tuple-element.126), channel_id=5, replica_groups=mesh['dp'=8,'expert'=4] {'dp'}, dimensions={1}, use_global_device_ids=true | all-gather | bytes 589824 | tf_op jit(solution)/shard_map/all_gather | solution.py:54
  118.6 4.3 all-to-all-start
  122.9 15.7 %all-gather.4 = bf16[1,512,8]{2,0,1:T(2,128)(2,1)S(1)} all-gather(bf16[1,64,8]{2,0,1:T(2,128)(2,1)} %copy.379), channel_id=6, replica_groups=mesh['dp'=8,'expert'=4] {'dp'}, dimensions={1}, use_global_device_ids=true | all-gather | bytes 9216 | tf_op jit(solution)/shard_map/all_gather | solution.py:55
  140.0 14.2 %all-gather.7 = bf16[1,2,512]{1,0,2:T(2,128)(2,1)S(1)} all-gather(bf16[1,2,64]{1,0,2:T(2,128)(2,1)S(1)} %copy.380), channel_id=9, replica_groups=mesh['dp'=8,'expert'=4] {'dp'}, dimensions={2}, use_global_device_ids=true | all-gather | bytes 2304 | tf_op jit(solution)/shard_map/all_gather | solution.py:56
  155.8 15.6 %all-gather.8 = bf16[1,2,512]{1,0,2:T(2,128)(2,1)S(1)} all-gather(bf16[1,2,64]{1,0,2:T(2,128)(2,1)} %copy.381), channel_id=10, replica_groups=mesh['dp'=8,'expert'=4] {'dp'}, dimensions={2}, use_global_device_ids=true | all-gather | bytes 2304 | tf_op jit(solution)/shard_map/all_gather | solution.py:57
  183.4 9.1 fusion.17
  192.5 6.6 fusion.77
  201.4 4.3 all-to-all-start.1
  206.3 17.5 %all-gather.10 = bf16[1,512,512]{2,1,0:T(8,128)(2,1)} all-gather(bf16[1,64,512]{2,1,0:T(8,128)(2,1)S(1)} %copy-done.50), channel_id=12, replica_groups=mesh['dp'=8,'expert'=4] {'dp'}, dimensions={1}, use_global_device_ids=true | all-gather | bytes 589824 | tf_op jit(solution)/shard_map/all_gather | solution.py:54
  230.6 4.3 gather_fusion
  234.9 4.1 gather_fusion.1
  242.0 4.1 fusion.213
  282.2 4.3 all-to-all-start.2
  287.3 14.8 %all-gather.11 = bf16[1,512,8]{2,0,1:T(2,128)(2,1)S(1)} all-gather(bf16[1,64,8]{2,0,1:T(2,128)(2,1)} %copy.382), channel_id=13, replica_groups=mesh['dp'=8,'expert'=4] {'dp'}, dimensions={1}, use_global_device_ids=true | all-gather | bytes 9216 | tf_op jit(solution)/shard_map/all_gather | solution.py:55
  306.9 9.1 fusion.13
  316.0 6.4 fusion.83
  324.8 4.3 all-to-all-start.3
  330.4 15.1 %all-to-all-done.3 = bf16[4,2,147,512]{3,1,2,0:T(2,128)(2,1)} async-done(((bf16[4,2,147,512]{3,1,2,0:T(2,128)(2,1)}), bf16[4,2,147,512]{3,1,2,0:T(2,128)(2,1)}, u32[]{:S(2)}, u32[]{:S(2)}) %all-to-all-start.3) | async-done | bytes 1204256 | tf_op jit(solution)/shard_map/all_to_all | solution.py:110
  354.7 4.0 gather_fusion.2
  369.8 18.9 %all_to_all.44 = bf16[4,2,147,512]{3,1,2,0:T(2,128)(2,1)S(1)} all-to-all(bf16[4,2,147,512]{3,1,2,0:T(2,128)(2,1)S(1)} %copy.295), channel_id=1, replica_groups=mesh['dp'=8,'expert'=4] {'expert'}, dimensions={0} | all-to-all | bytes 2408448 | tf_op jit(solution)/shard_map/all_to_all | solution.py:200
  388.7 8.1 fusion.5
  401.8 4.3 all-to-all-start.5
  406.2 14.4 %all-to-all-done.5 = bf16[4,2,147,512]{3,1,2,0:T(2,128)(2,1)} async-done(((bf16[4,2,147,512]{3,1,2,0:T(2,128)(2,1)}), bf16[4,2,147,512]{3,1,2,0:T(2,128)(2,1)}, u32[]{:S(2)}, u32[]{:S(2)}) %all-to-all-start.5) | async-done | bytes 1204256 | tf_op jit(solution)/shard_map/all_to_all | solution.py:214
  471.1 18.4 %all_to_all.45 = bf16[4,2,147,512]{3,1,2,0:T(2,128)(2,1)S(1)} all-to-all(bf16[4,2,147,512]{3,1,2,0:T(2,128)(2,1)S(1)} %copy.311), channel_id=1, replica_groups=mesh['dp'=8,'expert'=4] {'expert'}, dimensions={0} | all-to-all | bytes 2408448 | tf_op jit(solution)/shard_map/all_to_all | solution.py:200
  489.5 8.1 fusion.11
  502.6 4.4 all-to-all-start.7
  509.8 11.1 %all-to-all-done.7 = bf16[4,2,147,512]{3,1,2,0:T(2,128)(2,1)} async-done(((bf16[4,2,147,512]{3,1,2,0:T(2,128)(2,1)}), bf16[4,2,147,512]{3,1,2,0:T(2,128)(2,1)}, u32[]{:S(2)}, u32[]{:S(2)}) %all-to-all-start.7) | async-done | bytes 1204256 | tf_op jit(solution)/shard_map/all_to_all | solution.py:214
  532.0 4.1 convolution_convert_fusion
  569.2 5.1 reduce-scatter.39.cloned.1.call-done
  574.3 35.1 %reduce-scatter.37.cloned.1.call-done = bf16[64,1536]{1,0:T(8,128)(2,1)} async-done(((bf16[512,1536]{1,0:T(8,128)(2,1)}), bf16[64,1536]{1,0:T(8,128)(2,1)}) %reduce-scatter.37.cloned.1.call-update) | async-done | bytes 196624 | tf_op jit(solution)/shard_map/reduce_scatter | solution.py:322
  609.4 34.7 %reduce-scatter.35.cloned.1.call-done = bf16[64,1536]{1,0:T(8,128)(2,1)} async-done(((bf16[512,1536]{1,0:T(8,128)(2,1)}), bf16[64,1536]{1,0:T(8,128)(2,1)}) %reduce-scatter.35.cloned.1.call-update) | async-done | bytes 196624 | tf_op jit(solution)/shard_map/reduce_scatter | solution.py:322
  644.4 8.4 bitcast_convert_fusion
  654.0 8.5 bitcast_convert_fusion.1
  662.6 8.4 bitcast_convert_fusion.2
  671.3 8.3 bitcast_convert_fusion.3
  681.8 25.0 %reduce-scatter.53.cloned.1.call-done = bf16[64,2]{1,0:T(8,128)(2,1)} async-done(((bf16[512,2]{1,0:T(8,128)(2,1)}), bf16[64,2]{1,0:T(8,128)(2,1)}) %reduce-scatter.53.cloned.1.call-update) | async-done | bytes 272
  707.6 30.8 %reduce-scatter.49.cloned.1.call-done = bf16[64,2]{1,0:T(8,128)(2,1)} async-done(((bf16[512,2]{1,0:T(8,128)(2,1)}), bf16[64,2]{1,0:T(8,128)(2,1)}) %reduce-scatter.49.cloned.1.call-update) | async-done | bytes 272
  739.2 30.7 %reduce-scatter.43.cloned.1.call-done = bf16[64,8]{1,0:T(8,128)(2,1)} async-done(((bf16[512,8]{1,0:T(8,128)(2,1)}), bf16[64,8]{1,0:T(8,128)(2,1)}) %reduce-scatter.43.cloned.1.call-update) | async-done | bytes 1040
  772.6 28.1 %reduce-scatter.51.cloned.1.call-done = bf16[64,2]{1,0:T(8,128)(2,1)} async-done(((bf16[512,2]{1,0:T(8,128)(2,1)}), bf16[64,2]{1,0:T(8,128)(2,1)}) %reduce-scatter.51.cloned.1.call-update) | async-done | bytes 272
  801.5 30.6 %reduce-scatter.47.cloned.1.call-done = bf16[64,2]{1,0:T(8,128)(2,1)} async-done(((bf16[512,2]{1,0:T(8,128)(2,1)}), bf16[64,2]{1,0:T(8,128)(2,1)}) %reduce-scatter.47.cloned.1.call-update) | async-done | bytes 272
  832.9 10.1 all-reduce.2
  844.7 34.3 %all-reduce.6.cloned.1.call-done = (bf16[64,1536]{1,0:T(8,128)(2,1)}, bf16[64,1536]{1,0:T(8,128)(2,1)}, bf16[64,512]{1,0:T(8,128)(2,1)}, bf16[64,512]{1,0:T(8,128)(2,1)}) async-done(((bf16[64,1536]{1,0:T(8,128)(2,1)}, bf16[64,1536]{1,0:T(8,128)(2,1)}, bf16[64,512]{1,0:T(8,128)(2,1)}, bf16[64,512]{1,0:T(8,128)(2,1)}), (bf16[64,1536]{1,0:T(8,128)(2,1)}, bf16[64,1536]{1,0:T(8,128)(2,1)}, ...) | async-done | bytes 524304 | tf_op jit(solution)/shard_map/psum | solution.py:315
  882.6 48.5 %reduce-scatter.33.cloned.1.call-done = bf16[2,256,512]{2,1,0:T(8,128)(2,1)} async-done(((bf16[2,2048,512]{2,1,0:T(8,128)(2,1)}), bf16[2,256,512]{2,1,0:T(8,128)(2,1)}) %reduce-scatter.33.cloned.1.call-update) | async-done | bytes 524304 | tf_op jit(solution)/shard_map/reduce_scatter | solution.py:342
  931.1 50.7 %reduce-scatter.31.cloned.1.call-done = bf16[2,256,512]{2,1,0:T(8,128)(2,1)} async-done(((bf16[2,2048,512]{2,1,0:T(8,128)(2,1)}), bf16[2,256,512]{2,1,0:T(8,128)(2,1)}) %reduce-scatter.31.cloned.1.call-update) | async-done | bytes 524304 | tf_op jit(solution)/shard_map/reduce_scatter | solution.py:342
  984.5 47.9 %reduce-scatter.29.cloned.1.call-done = bf16[2,512,256]{2,1,0:T(8,128)(2,1)} async-done(((bf16[2,512,2048]{2,1,0:T(8,128)(2,1)}), bf16[2,512,256]{2,1,0:T(8,128)(2,1)}) %reduce-scatter.29.cloned.1.call-update) | async-done | bytes 524304 | tf_op jit(solution)/shard_map/reduce_scatter | solution.py:339
  1032.4 50.7 %reduce-scatter.27.cloned.1.call-done = bf16[2,512,256]{2,1,0:T(8,128)(2,1)} async-done(((bf16[2,512,2048]{2,1,0:T(8,128)(2,1)}), bf16[2,512,256]{2,1,0:T(8,128)(2,1)}) %reduce-scatter.27.cloned.1.call-update) | async-done | bytes 524304 | tf_op jit(solution)/shard_map/reduce_scatter | solution.py:339
  (571 shorter events, 274.2 us)
Async XLA Ops:
  7.2 80.8 %all-gather.21.cloned.1.call-start = ((), (), s32[]{:S(2)}) async-start(), calls=%async_computation.26 | async-start | bytes 1769472 | tf_op jit(solution)/shard_map/all_gather | solution.py:53
  9.1 174.3 %all-gather.23.cloned.1.call-start = ((), (), s32[]{:S(2)}) async-start(), calls=%async_computation.27 | async-start | bytes 4718592 | tf_op jit(solution)/shard_map/all_gather | solution.py:60
  11.5 181.1 %all-gather.25.cloned.1.call-start = ((), (), s32[]{:S(2)}) async-start(), calls=%async_computation.28 | async-start | bytes 4718592 | tf_op jit(solution)/shard_map/all_gather | solution.py:61
  12.6 229.4 %all-gather.27.cloned.1.call-start = ((), (), s32[]{:S(2)}) async-start(), calls=%async_computation.29 | async-start | bytes 1769472 | tf_op jit(solution)/shard_map/all_gather | solution.py:53
  13.2 293.7 %all-gather.29.cloned.1.call-start = ((), (), s32[]{:S(2)}) async-start(), calls=%async_computation.30 | async-start | bytes 4718592 | tf_op jit(solution)/shard_map/all_gather | solution.py:60
  13.8 302.3 %all-gather.31.cloned.1.call-start = ((), (), s32[]{:S(2)}) async-start(), calls=%async_computation.31 | async-start | bytes 4718592 | tf_op jit(solution)/shard_map/all_gather | solution.py:61
  14.5 22.5 %copy-start.132 = (bf16[2,2,64]{2,1,0:T(2,128)(2,1)S(1)}, bf16[2,2,64]{2,1,0:T(2,128)(2,1)}, u32[]{:S(2)}) copy-start(bf16[2,2,64]{2,1,0:T(2,128)(2,1)} %param.18) | copy-start | bytes 1540
  15.7 39.6 %copy-start.57 = (bf16[2,64,512]{2,1,0:T(8,128)(2,1)S(1)}, bf16[2,64,512]{2,1,0:T(8,128)(2,1)}, u32[]{:S(2)}) copy-start(bf16[2,64,512]{2,1,0:T(8,128)(2,1)} %param.15) | copy-start | bytes 393220
  33.8 47.3 %copy-start.110 = (s32[2,2,197,2]{2,3,1,0:T(2,128)S(1)}, s32[2,2,197,2]{2,3,1,0:T(2,128)}, u32[]{:S(2)}) copy-start(s32[2,2,197,2]{2,3,1,0:T(2,128)} %param.21) | copy-start | bytes 18916
  33.9 50.2 %copy-start.130 = (bf16[2,64,8]{1,2,0:T(8,128)(2,1)S(1)}, bf16[2,64,8]{1,2,0:T(8,128)(2,1)}, u32[]{:S(2)}) copy-start(bf16[2,64,8]{1,2,0:T(8,128)(2,1)} %param.16) | copy-start | bytes 6148
  36.6 53.7 %copy-start.94 = (f32[512]{0:T(512)}, f32[512]{0:T(512)S(1)}, u32[]{:S(2)}) copy-start(f32[512]{0:T(512)S(1)} %get-tuple-element.80) | copy-start | bytes 6148
  36.6 72.6 %copy-start.100 = (f32[512]{0:T(512)}, f32[512]{0:T(512)S(1)}, u32[]{:S(2)}) copy-start(f32[512]{0:T(512)S(1)} %get-tuple-element.79) | copy-start | bytes 6148
  36.7 53.6 %copy-start.8 = (f32[394,512]{1,0:T(8,128)}, f32[394,512]{1,0:T(8,128)S(1)}, u32[]{:S(2)}) copy-start(f32[394,512]{1,0:T(8,128)S(1)} %reshape.331) | copy-start | bytes 2420740
  36.9 53.4 %copy-start.78 = (f32[394]{0:T(512)}, f32[394]{0:T(512)S(1)}, u32[]{:S(2)}) copy-start(f32[394]{0:T(512)S(1)} %rsqrt.40) | copy-start | bytes 4732
  37.0 53.3 %copy-start.80 = (f32[394]{0:T(512)}, f32[394]{0:T(512)S(1)}, u32[]{:S(2)}) copy-start(f32[394]{0:T(512)S(1)} %div.51) | copy-start | bytes 4732
  55.3 35.1 %copy-start.104 = (f32[512]{0:T(512)}, f32[512]{0:T(512)S(1)}, u32[]{:S(2)}) copy-start(f32[512]{0:T(512)S(1)} %get-tuple-element.82) | copy-start | bytes 6148
  83.4 26.6 %copy-start.116 = (s32[394]{0:T(512)}, s32[394]{0:T(512)S(1)}, u32[]{:S(2)}) copy-start(s32[394]{0:T(512)S(1)} %get-tuple-element.110) | copy-start | bytes 4732
  83.4 26.6 %copy-start.118 = (s32[394]{0:T(512)}, s32[394]{0:T(512)S(1)}, u32[]{:S(2)}) copy-start(s32[394]{0:T(512)S(1)} %get-tuple-element.168) | copy-start | bytes 4732
  118.6 64.8 %all-to-all-start = ((bf16[4,2,147,512]{3,1,2,0:T(2,128)(2,1)}), bf16[4,2,147,512]{3,1,2,0:T(2,128)(2,1)}, u32[]{:S(2)}, u32[]{:S(2)}) async-start(bf16[4,2,147,512]{3,1,2,0:T(2,128)(2,1)} %copy.273), calls=%async_computation | async-start | bytes 2408448 | tf_op jit(solution)/shard_map/all_to_all | solution.py:102
  182.2 59.8 %copy-start.106 = (f32[512]{0:T(512)}, f32[512]{0:T(512)S(1)}, u32[]{:S(2)}) copy-start(f32[512]{0:T(512)S(1)} %get-tuple-element.78) | copy-start | bytes 6148
  183.4 90.3 %copy-start.112 = (s32[394]{0:T(512)}, s32[394]{0:T(512)S(1)}, u32[]{:S(2)}) copy-start(s32[394]{0:T(512)S(1)} %get-tuple-element.104) | copy-start | bytes 4732
  199.1 24.7 %copy-start.71 = (bf16[1,512,8]{1,2,0:T(8,128)(2,1)S(1)}, bf16[1,512,8]{1,2,0:T(8,128)(2,1)}, u32[]{:S(2)}) copy-start(bf16[1,512,8]{1,2,0:T(8,128)(2,1)} %copy.271) | copy-start | bytes 24580
  199.1 26.0 %copy-start.59 = (s32[394,1]{0,1:T(1,128)S(1)}, s32[394,1]{0,1:T(1,128)}, u32[]{:S(2)}) copy-start(s32[394,1]{0,1:T(1,128)} %copy-done.58) | copy-start | bytes 4732
  199.2 26.0 %copy-start.62 = (s32[394,1]{0,1:T(1,128)S(1)}, s32[394,1]{0,1:T(1,128)}, u32[]{:S(2)}) copy-start(s32[394,1]{0,1:T(1,128)} %copy-done.61) | copy-start | bytes 4732
  201.4 23.8 %all-to-all-start.1 = ((bf16[4,2,147,512]{3,1,2,0:T(2,128)(2,1)}), bf16[4,2,147,512]{3,1,2,0:T(2,128)(2,1)}, u32[]{:S(2)}, u32[]{:S(2)}) async-start(bf16[4,2,147,512]{3,1,2,0:T(2,128)(2,1)} %copy.275), calls=%async_computation.1 | async-start | bytes 2408448 | tf_op jit(solution)/shard_map/all_to_all | solution.py:110
  206.3 67.3 %copy-start.114 = (s32[394]{0:T(512)}, s32[394]{0:T(512)S(1)}, u32[]{:S(2)}) copy-start(s32[394]{0:T(512)S(1)} %get-tuple-element.106) | copy-start | bytes 4732
  282.2 24.7 %all-to-all-start.2 = ((bf16[4,2,147,512]{3,1,2,0:T(2,128)(2,1)}), bf16[4,2,147,512]{3,1,2,0:T(2,128)(2,1)}, u32[]{:S(2)}, u32[]{:S(2)}) async-start(bf16[4,2,147,512]{3,1,2,0:T(2,128)(2,1)} %copy.290), calls=%async_computation.2 | async-start | bytes 2408448 | tf_op jit(solution)/shard_map/all_to_all | solution.py:102
  324.8 20.7 %all-to-all-start.3 = ((bf16[4,2,147,512]{3,1,2,0:T(2,128)(2,1)}), bf16[4,2,147,512]{3,1,2,0:T(2,128)(2,1)}, u32[]{:S(2)}, u32[]{:S(2)}) async-start(bf16[4,2,147,512]{3,1,2,0:T(2,128)(2,1)} %copy.292), calls=%async_computation.3 | async-start | bytes 2408448 | tf_op jit(solution)/shard_map/all_to_all | solution.py:110
  367.4 21.2 %copy-start.136 = (bf16[1,2,2048,512]{3,2,1,0:T(8,128)(2,1)S(1)}, bf16[1,2,2048,512]{3,2,1,0:T(8,128)(2,1)}, u32[]{:S(2)}) copy-start(bf16[1,2,2048,512]{3,2,1,0:T(8,128)(2,1)} %all-gather.31.cloned.1.call-done) | copy-start | bytes 12582916
  401.8 18.8 %all-to-all-start.5 = ((bf16[4,2,147,512]{3,1,2,0:T(2,128)(2,1)}), bf16[4,2,147,512]{3,1,2,0:T(2,128)(2,1)}, u32[]{:S(2)}, u32[]{:S(2)}) async-start(bf16[4,2,147,512]{3,1,2,0:T(2,128)(2,1)} %copy.297), calls=%async_computation.5 | async-start | bytes 2408448 | tf_op jit(solution)/shard_map/all_to_all | solution.py:214
  502.6 18.2 %all-to-all-start.7 = ((bf16[4,2,147,512]{3,1,2,0:T(2,128)(2,1)}), bf16[4,2,147,512]{3,1,2,0:T(2,128)(2,1)}, u32[]{:S(2)}, u32[]{:S(2)}) async-start(bf16[4,2,147,512]{3,1,2,0:T(2,128)(2,1)} %copy.313), calls=%async_computation.7 | async-start | bytes 2408448 | tf_op jit(solution)/shard_map/all_to_all | solution.py:214
  507.1 62.2 %reduce-scatter.41.cloned.1.call-start = ((), (), s32[]{:S(2)}) async-start(), calls=%async_computation.35 | async-start | bytes 589824 | tf_op jit(solution)/shard_map/reduce_scatter | solution.py:325
  509.7 64.6 %reduce-scatter.39.cloned.1.call-start = ((), (), s32[]{:S(2)}) async-start(), calls=%async_computation.34 | async-start | bytes 589824 | tf_op jit(solution)/shard_map/reduce_scatter | solution.py:325
  532.0 77.4 %reduce-scatter.37.cloned.1.call-start = ((), (), s32[]{:S(2)}) async-start(), calls=%async_computation.33 | async-start | bytes 1769472 | tf_op jit(solution)/shard_map/reduce_scatter | solution.py:322
  536.1 108.0 %reduce-scatter.35.cloned.1.call-start = ((), (), s32[]{:S(2)}) async-start(), calls=%async_computation.32 | async-start | bytes 1769472 | tf_op jit(solution)/shard_map/reduce_scatter | solution.py:322
  560.0 119.7 %reduce-scatter.45.cloned.1.call-start = ((), (), s32[]{:S(2)}) async-start(), calls=%async_computation.37 | async-start | bytes 147456
  561.0 145.8 %reduce-scatter.53.cloned.1.call-start = ((), (), s32[]{:S(2)}) async-start(), calls=%async_computation.41 | async-start | bytes 147456
  561.9 176.5 %reduce-scatter.49.cloned.1.call-start = ((), (), s32[]{:S(2)}) async-start(), calls=%async_computation.39 | async-start | bytes 147456
  562.9 207.0 %reduce-scatter.43.cloned.1.call-start = ((), (), s32[]{:S(2)}) async-start(), calls=%async_computation.36 | async-start | bytes 147456
  563.9 236.8 %reduce-scatter.51.cloned.1.call-start = ((), (), s32[]{:S(2)}) async-start(), calls=%async_computation.40 | async-start | bytes 147456
  568.2 263.8 %reduce-scatter.47.cloned.1.call-start = ((), (), s32[]{:S(2)}) async-start(), calls=%async_computation.38 | async-start | bytes 147456
  569.1 309.9 %all-reduce.6.cloned.1.call-start = ((), (), s32[]{:S(2)}) async-start(), calls=%async_computation.42 | async-start | bytes 1048576 | tf_op jit(solution)/shard_map/psum | solution.py:315
  644.1 287.0 %reduce-scatter.33.cloned.1.call-start = ((), (), s32[]{:S(2)}) async-start(), calls=%async_computation.25 | async-start | bytes 4718592 | tf_op jit(solution)/shard_map/reduce_scatter | solution.py:342
  652.8 329.1 %reduce-scatter.31.cloned.1.call-start = ((), (), s32[]{:S(2)}) async-start(), calls=%async_computation.24 | async-start | bytes 4718592 | tf_op jit(solution)/shard_map/reduce_scatter | solution.py:342
  662.6 369.8 %reduce-scatter.29.cloned.1.call-start = ((), (), s32[]{:S(2)}) async-start(), calls=%async_computation.23 | async-start | bytes 4718592 | tf_op jit(solution)/shard_map/reduce_scatter | solution.py:339
  671.0 412.1 %reduce-scatter.27.cloned.1.call-start = ((), (), s32[]{:S(2)}) async-start(), calls=%async_computation.22 | async-start | bytes 4718592 | tf_op jit(solution)/shard_map/reduce_scatter | solution.py:339
  679.6 91.0 %copy-start.13 = (f32[394,512]{1,0:T(8,128)S(1)}, f32[394,512]{1,0:T(8,128)}, u32[]{:S(2)}) copy-start(f32[394,512]{1,0:T(8,128)} %copy-done.12) | copy-start | bytes 2420740
  679.6 91.0 %copy-start.49 = (f32[394,512]{1,0:T(8,128)S(1)}, f32[394,512]{1,0:T(8,128)}, u32[]{:S(2)}) copy-start(f32[394,512]{1,0:T(8,128)} %get-tuple-element.166) | copy-start | bytes 2420740
  (118 other events, 428.8 us)
Sparse Core Ops, SparseCore 0:
  10.2 29.4 all-gather.20
  41.3 51.4 all-gather.22
  94.4 47.3 all-gather.24
  143.9 25.8 all-gather.26
  171.2 49.7 all-gather.28
  222.4 45.8 all-gather.30
  510.1 32.3 reduce-scatter.40
  544.8 29.4 reduce-scatter.38
  577.2 32.1 reduce-scatter.36
  611.6 32.4 reduce-scatter.34
  646.9 28.9 reduce-scatter.44
  678.1 28.7 reduce-scatter.52
  709.6 28.7 reduce-scatter.48
  741.1 28.7 reduce-scatter.42
  771.9 28.7 reduce-scatter.50
  803.4 28.6 reduce-scatter.46
  835.2 43.8 all-reduce.5
  881.2 49.8 reduce-scatter.32
  933.4 48.3 reduce-scatter.30
  984.0 48.3 reduce-scatter.28
  1034.7 48.3 reduce-scatter.26
where the time goes:
time: 1100 us; the launch traced here: 1090 us
  waiting for transfers between devices  495 us (45%)
  local copies, waits for them, and re-layouts  186 us (17%)
  blocking collectives  182 us (17%)
  matrix products  151 us (14%)
  other arithmetic  35 us (3%)
  starting transfers between devices  27.2 us (2%)
  between operations  16.6 us (2%)
    unnamed x27, waiting for transfers between devices  147 us
    reduce_scatter x2, waiting for transfers between devices, body(): lax.psum_scatter(expert_part[1].astype(jnp.bfloat16), 'dp', scatter_dimen...  99.3 us
    reduce_scatter x2, waiting for transfers between devices, body(): lax.psum_scatter(expert_part[0].astype(jnp.bfloat16), 'dp', scatter_dimen...  98.6 us
    reduce_scatter x2, waiting for transfers between devices, body(): lax.psum_scatter(totals[0].astype(jnp.bfloat16), 'dp', scatter_dimension=...  69.8 us
    all_gather x2, blocking collectives, layer_forward(): lax.all_gather(w_proj[which], 'dp', axis=0, tiled=True)  42.8 us
    all_to_all x2, blocking collectives, layer_backward(): lax.all_to_all(slot_grads, 'expert', split_axis=0, concat_axis=0, tiled=T...  37.3 us
    psum x1, waiting for transfers between devices, body(): lax.psum(dense[0].astype(jnp.bfloat16), 'expert').astype(jnp.float32)  34.3 us
    unnamed x304, local copies, waits for them, and re-layouts  32.4 us
  transfers between devices with their start and end apart: 27, of which 16 were waited for; matrix products, arithmetic and copies ran while one was open for 23% of the time, Pallas kernels for 0%

commit v1 on v0

--- a/solution.py
+++ b/solution.py
@@ -12,6 +12,28 @@
 INV_ROOT_TAU = 0.3989422804014327
 
 
+def laid_out(pieces, dim):
+    lengths = list(pieces.shape[1:])
+    lengths[dim] *= pieces.shape[0]
+    return jnp.moveaxis(pieces, 0, dim).reshape(lengths)
+
+
+def grow_blocks(array, axis):
+    devices = lax.axis_size(axis)
+    blocks = array[None]
+    for level in range(devices.bit_length() - 1):
+        bit = 1 << level
+        other = lax.ppermute(blocks, axis, [(i, i ^ bit) for i in range(devices)])
+        both = jnp.stack([blocks, other])
+        upper = lax.axis_index(axis) >> level & 1
+        blocks = jnp.where(upper == 0, both, both[::-1]).reshape(-1, *array.shape)
+    return blocks
+
+
+def doubled_up(value, axis, dim):
+    return laid_out(grow_blocks(value, axis), dim)
+
+
 def layer_norm(values, scale_in, shift_in):
     center = values - jnp.mean(values, axis=-1, keepdims=True)
     variance = jnp.mean(center * center, axis=-1, keepdims=True)
@@ -51,7 +73,7 @@
 ):
     qkv_full, proj_full, router_full, gains_full, shifts_full = (
         lax.all_gather(w_qkv[which], "dp", axis=0, tiled=True),
-        lax.all_gather(w_proj[which], "dp", axis=0, tiled=True),
+        doubled_up(w_proj[which], "dp", 0),
         lax.all_gather(w_router[which], "dp", axis=0, tiled=True),
         lax.all_gather(norm_gains[which], "dp", axis=1, tiled=True),
         lax.all_gather(norm_shifts[which], "dp", axis=1, tiled=True),

time: 1100 us -> 1100 us (level)
  blocking collectives: 182 us -> 155 us
  waiting for transfers between devices: 495 us -> 509 us
    all_gather x2 -> x0, blocking collectives: 42.8 us -> none  [layer_forward(): lax.all_gather(w_proj[which], 'dp', axis=0, tiled=True)]
    ppermute x0 -> x6, waiting for transfers between devices: none -> 11.1 us  [grow_blocks(): other = lax.ppermute(blocks, axis, [(i, i ^ bit) for i in range(devices)])]
    unnamed x304 -> x310, local copies, waits for them, and re-layouts: 32.4 us -> 30.6 us
  transfers between devices with their start and end apart: 27 -> 33, of which waited for: 16 -> 19; matrix products, arithmetic and copies ran while one was open for 23% -> 23% of each run, Pallas kernels for 0% -> 0%
where the time goes in v1:
time: 1100 us; the launch traced here: 1090 us
  waiting for transfers between devices  509 us (46%)
  local copies, waits for them, and re-layouts  183 us (17%)
  blocking collectives  155 us (14%)
  matrix products  151 us (14%)
  other arithmetic  38.4 us (3%)
  starting transfers between devices  34.7 us (3%)
  between operations  16.7 us (2%)
    unnamed x27, waiting for transfers between devices  147 us
    reduce_scatter x2, waiting for transfers between devices, body(): lax.psum_scatter(expert_part[1].astype(jnp.bfloat16), 'dp', scatter_dimen...  99.3 us
    reduce_scatter x2, waiting for transfers between devices, body(): lax.psum_scatter(expert_part[0].astype(jnp.bfloat16), 'dp', scatter_dimen...  98.6 us
    reduce_scatter x2, waiting for transfers between devices, body(): lax.psum_scatter(totals[0].astype(jnp.bfloat16), 'dp', scatter_dimension=...  70.1 us
    all_gather x2, blocking collectives, layer_forward(): lax.all_gather(norm_gains[which], 'dp', axis=1, tiled=True)  40.4 us
    all_to_all x2, blocking collectives, layer_backward(): lax.all_to_all(slot_grads, 'expert', split_axis=0, concat_axis=0, tiled=T...  36.9 us
    all_gather x2, blocking collectives, layer_forward(): lax.all_gather(norm_shifts[which], 'dp', axis=1, tiled=True)  35.8 us
    psum x1, waiting for transfers between devices, body(): lax.psum(dense[0].astype(jnp.bfloat16), 'expert').astype(jnp.float32)  34.4 us
  transfers between devices with their start and end apart: 33, of which 19 were waited for; matrix products, arithmetic and copies ran while one was open for 23% of the time, Pallas kernels for 0%

profile of v1, /device:TPU:0, one launch (start us, length us, event | category | flops | bytes accessed | tf_op | source)
XLA Modules:
  0.0 1086.9 jit_solution(1104849088516114280)
XLA Ops:
  15.2 16.9 %all-gather = bf16[1,2,512]{1,0,2:T(2,128)(2,1)S(1)} all-gather(bf16[1,2,64]{1,0,2:T(2,128)(2,1)S(1)} %copy.387), channel_id=2, replica_groups=mesh['dp'=8,'expert'=4] {'dp'}, dimensions={2}, use_global_device_ids=true | all-gather | bytes 2304 | tf_op jit(solution)/shard_map/all_gather | solution.py:78
  42.8 15.4 %all-gather.1 = bf16[1,2,512]{1,0,2:T(2,128)(2,1)S(1)} all-gather(bf16[1,2,64]{1,0,2:T(2,128)(2,1)S(1)} %copy.388), channel_id=3, replica_groups=mesh['dp'=8,'expert'=4] {'dp'}, dimensions={2}, use_global_device_ids=true | all-gather | bytes 2304 | tf_op jit(solution)/shard_map/all_gather | solution.py:79
  58.6 23.5 %all-gather.6 = bf16[1,2,512]{1,0,2:T(2,128)(2,1)S(1)} all-gather(bf16[1,2,64]{1,0,2:T(2,128)(2,1)S(1)} %copy.390), channel_id=8, replica_groups=mesh['dp'=8,'expert'=4] {'dp'}, dimensions={2}, use_global_device_ids=true | all-gather | bytes 2304 | tf_op jit(solution)/shard_map/all_gather | solution.py:78
  98.5 20.4 %all-gather.7 = bf16[1,2,512]{1,0,2:T(2,128)(2,1)S(1)} all-gather(bf16[1,2,64]{1,0,2:T(2,128)(2,1)S(1)} %copy.391), channel_id=9, replica_groups=mesh['dp'=8,'expert'=4] {'dp'}, dimensions={2}, use_global_device_ids=true | all-gather | bytes 2304 | tf_op jit(solution)/shard_map/all_gather | solution.py:79
  151.2 4.9 all-to-all-start
  161.8 17.3 %all-gather.3 = bf16[1,512,8]{2,0,1:T(2,128)(2,1)S(1)} all-gather(bf16[1,64,8]{2,0,1:T(2,128)(2,1)} %copy.389), channel_id=5, replica_groups=mesh['dp'=8,'expert'=4] {'dp'}, dimensions={1}, use_global_device_ids=true | all-gather | bytes 9216 | tf_op jit(solution)/shard_map/all_gather | solution.py:77
  182.0 9.4 fusion.17
  191.5 6.6 fusion.77
  200.4 4.3 all-to-all-start.1
  205.3 7.9 collective-permute-done.5
  216.5 4.0 all-to-all-done.1
  225.8 4.0 gather_fusion
  229.8 4.0 gather_fusion.1
  237.0 4.0 fusion.212
  277.5 4.3 all-to-all-start.2
  282.5 14.5 %all-gather.9 = bf16[1,512,8]{2,0,1:T(2,128)(2,1)S(1)} all-gather(bf16[1,64,8]{2,0,1:T(2,128)(2,1)} %copy.392), channel_id=11, replica_groups=mesh['dp'=8,'expert'=4] {'dp'}, dimensions={1}, use_global_device_ids=true | all-gather | bytes 9216 | tf_op jit(solution)/shard_map/all_gather | solution.py:77
  301.8 9.0 fusion.13
  310.9 6.4 fusion.83
  319.6 4.7 all-to-all-start.3
  325.6 15.0 %all-to-all-done.3 = bf16[4,2,147,512]{3,1,2,0:T(2,128)(2,1)} async-done(((bf16[4,2,147,512]{3,1,2,0:T(2,128)(2,1)}), bf16[4,2,147,512]{3,1,2,0:T(2,128)(2,1)}, u32[]{:S(2)}, u32[]{:S(2)}) %all-to-all-start.3) | async-done | bytes 1204256 | tf_op jit(solution)/shard_map/all_to_all | solution.py:132
  345.8 4.0 gather_fusion.3
  349.9 4.0 gather_fusion.2
  364.9 18.6 %all_to_all.44 = bf16[4,2,147,512]{3,1,2,0:T(2,128)(2,1)S(1)} all-to-all(bf16[4,2,147,512]{3,1,2,0:T(2,128)(2,1)S(1)} %copy.305), channel_id=1, replica_groups=mesh['dp'=8,'expert'=4] {'expert'}, dimensions={0} | all-to-all | bytes 2408448 | tf_op jit(solution)/shard_map/all_to_all | solution.py:222
  383.5 8.1 fusion.5
  396.7 4.4 all-to-all-start.5
  401.2 14.4 %all-to-all-done.5 = bf16[4,2,147,512]{3,1,2,0:T(2,128)(2,1)} async-done(((bf16[4,2,147,512]{3,1,2,0:T(2,128)(2,1)}), bf16[4,2,147,512]{3,1,2,0:T(2,128)(2,1)}, u32[]{:S(2)}, u32[]{:S(2)}) %all-to-all-start.5) | async-done | bytes 1204256 | tf_op jit(solution)/shard_map/all_to_all | solution.py:236
  465.9 18.3 %all_to_all.45 = bf16[4,2,147,512]{3,1,2,0:T(2,128)(2,1)S(1)} all-to-all(bf16[4,2,147,512]{3,1,2,0:T(2,128)(2,1)S(1)} %copy.321), channel_id=1, replica_groups=mesh['dp'=8,'expert'=4] {'expert'}, dimensions={0} | all-to-all | bytes 2408448 | tf_op jit(solution)/shard_map/all_to_all | solution.py:222
  484.1 8.1 fusion.11
  497.3 4.3 all-to-all-start.7
  504.3 11.1 %all-to-all-done.7 = bf16[4,2,147,512]{3,1,2,0:T(2,128)(2,1)} async-done(((bf16[4,2,147,512]{3,1,2,0:T(2,128)(2,1)}), bf16[4,2,147,512]{3,1,2,0:T(2,128)(2,1)}, u32[]{:S(2)}, u32[]{:S(2)}) %all-to-all-start.7) | async-done | bytes 1204256 | tf_op jit(solution)/shard_map/all_to_all | solution.py:236
  526.7 4.1 convolution_convert_fusion
  568.0 35.3 %reduce-scatter.37.cloned.1.call-done = bf16[64,1536]{1,0:T(8,128)(2,1)} async-done(((bf16[512,1536]{1,0:T(8,128)(2,1)}), bf16[64,1536]{1,0:T(8,128)(2,1)}) %reduce-scatter.37.cloned.1.call-update) | async-done | bytes 196624 | tf_op jit(solution)/shard_map/reduce_scatter | solution.py:344
  603.3 34.7 %reduce-scatter.35.cloned.1.call-done = bf16[64,1536]{1,0:T(8,128)(2,1)} async-done(((bf16[512,1536]{1,0:T(8,128)(2,1)}), bf16[64,1536]{1,0:T(8,128)(2,1)}) %reduce-scatter.35.cloned.1.call-update) | async-done | bytes 196624 | tf_op jit(solution)/shard_map/reduce_scatter | solution.py:344
  638.3 8.4 bitcast_convert_fusion
  648.0 8.5 bitcast_convert_fusion.1
  656.6 8.4 bitcast_convert_fusion.2
  665.2 8.3 bitcast_convert_fusion.3
  675.7 25.1 %reduce-scatter.53.cloned.1.call-done = bf16[64,2]{1,0:T(8,128)(2,1)} async-done(((bf16[512,2]{1,0:T(8,128)(2,1)}), bf16[64,2]{1,0:T(8,128)(2,1)}) %reduce-scatter.53.cloned.1.call-update) | async-done | bytes 272
  701.6 30.7 %reduce-scatter.49.cloned.1.call-done = bf16[64,2]{1,0:T(8,128)(2,1)} async-done(((bf16[512,2]{1,0:T(8,128)(2,1)}), bf16[64,2]{1,0:T(8,128)(2,1)}) %reduce-scatter.49.cloned.1.call-update) | async-done | bytes 272
  733.1 30.7 %reduce-scatter.43.cloned.1.call-done = bf16[64,8]{1,0:T(8,128)(2,1)} async-done(((bf16[512,8]{1,0:T(8,128)(2,1)}), bf16[64,8]{1,0:T(8,128)(2,1)}) %reduce-scatter.43.cloned.1.call-update) | async-done | bytes 1040
  766.5 28.1 %reduce-scatter.51.cloned.1.call-done = bf16[64,2]{1,0:T(8,128)(2,1)} async-done(((bf16[512,2]{1,0:T(8,128)(2,1)}), bf16[64,2]{1,0:T(8,128)(2,1)}) %reduce-scatter.51.cloned.1.call-update) | async-done | bytes 272
  795.4 30.7 %reduce-scatter.47.cloned.1.call-done = bf16[64,2]{1,0:T(8,128)(2,1)} async-done(((bf16[512,2]{1,0:T(8,128)(2,1)}), bf16[64,2]{1,0:T(8,128)(2,1)}) %reduce-scatter.47.cloned.1.call-update) | async-done | bytes 272
  826.8 10.1 all-reduce.2
  838.7 34.4 %all-reduce.6.cloned.1.call-done = (bf16[64,1536]{1,0:T(8,128)(2,1)}, bf16[64,1536]{1,0:T(8,128)(2,1)}, bf16[64,512]{1,0:T(8,128)(2,1)}, bf16[64,512]{1,0:T(8,128)(2,1)}) async-done(((bf16[64,1536]{1,0:T(8,128)(2,1)}, bf16[64,1536]{1,0:T(8,128)(2,1)}, bf16[64,512]{1,0:T(8,128)(2,1)}, bf16[64,512]{1,0:T(8,128)(2,1)}), (bf16[64,1536]{1,0:T(8,128)(2,1)}, bf16[64,1536]{1,0:T(8,128)(2,1)}, ...) | async-done | bytes 524304 | tf_op jit(solution)/shard_map/psum | solution.py:337
  876.6 48.5 %reduce-scatter.33.cloned.1.call-done = bf16[2,256,512]{2,1,0:T(8,128)(2,1)} async-done(((bf16[2,2048,512]{2,1,0:T(8,128)(2,1)}), bf16[2,256,512]{2,1,0:T(8,128)(2,1)}) %reduce-scatter.33.cloned.1.call-update) | async-done | bytes 524304 | tf_op jit(solution)/shard_map/reduce_scatter | solution.py:364
  925.1 50.7 %reduce-scatter.31.cloned.1.call-done = bf16[2,256,512]{2,1,0:T(8,128)(2,1)} async-done(((bf16[2,2048,512]{2,1,0:T(8,128)(2,1)}), bf16[2,256,512]{2,1,0:T(8,128)(2,1)}) %reduce-scatter.31.cloned.1.call-update) | async-done | bytes 524304 | tf_op jit(solution)/shard_map/reduce_scatter | solution.py:364
  978.5 47.9 %reduce-scatter.29.cloned.1.call-done = bf16[2,512,256]{2,1,0:T(8,128)(2,1)} async-done(((bf16[2,512,2048]{2,1,0:T(8,128)(2,1)}), bf16[2,512,256]{2,1,0:T(8,128)(2,1)}) %reduce-scatter.29.cloned.1.call-update) | async-done | bytes 524304 | tf_op jit(solution)/shard_map/reduce_scatter | solution.py:361
  1026.4 50.7 %reduce-scatter.27.cloned.1.call-done = bf16[2,512,256]{2,1,0:T(8,128)(2,1)} async-done(((bf16[2,512,2048]{2,1,0:T(8,128)(2,1)}), bf16[2,512,256]{2,1,0:T(8,128)(2,1)}) %reduce-scatter.27.cloned.1.call-update) | async-done | bytes 524304 | tf_op jit(solution)/shard_map/reduce_scatter | solution.py:361
  (599 shorter events, 283.1 us)
Async XLA Ops:
  7.2 113.5 %all-gather.19.cloned.1.call-start = ((), (), s32[]{:S(2)}) async-start(), calls=%async_computation.26 | async-start | bytes 1769472 | tf_op jit(solution)/shard_map/all_gather | solution.py:75
  9.1 172.9 %all-gather.21.cloned.1.call-start = ((), (), s32[]{:S(2)}) async-start(), calls=%async_computation.27 | async-start | bytes 4718592 | tf_op jit(solution)/shard_map/all_gather | solution.py:82
  11.4 180.0 %all-gather.23.cloned.1.call-start = ((), (), s32[]{:S(2)}) async-start(), calls=%async_computation.28 | async-start | bytes 4718592 | tf_op jit(solution)/shard_map/all_gather | solution.py:83
  12.6 21.1 %copy-start.135 = (bf16[2,2,64]{2,1,0:T(2,128)(2,1)S(1)}, bf16[2,2,64]{2,1,0:T(2,128)(2,1)}, u32[]{:S(2)}) copy-start(bf16[2,2,64]{2,1,0:T(2,128)(2,1)} %param.18) | copy-start | bytes 1540
  12.6 21.1 %copy-start.110 = (s32[2,2,197,2]{2,3,1,0:T(2,128)S(1)}, s32[2,2,197,2]{2,3,1,0:T(2,128)}, u32[]{:S(2)}) copy-start(s32[2,2,197,2]{2,3,1,0:T(2,128)} %param.21) | copy-start | bytes 18916
  12.6 23.9 %copy-start.133 = (bf16[2,64,8]{1,2,0:T(8,128)(2,1)S(1)}, bf16[2,64,8]{1,2,0:T(8,128)(2,1)}, u32[]{:S(2)}) copy-start(bf16[2,64,8]{1,2,0:T(8,128)(2,1)} %param.16) | copy-start | bytes 6148
  12.6 224.3 %all-gather.25.cloned.1.call-start = ((), (), s32[]{:S(2)}) async-start(), calls=%async_computation.29 | async-start | bytes 1769472 | tf_op jit(solution)/shard_map/all_gather | solution.py:75
  13.2 288.6 %all-gather.27.cloned.1.call-start = ((), (), s32[]{:S(2)}) async-start(), calls=%async_computation.30 | async-start | bytes 4718592 | tf_op jit(solution)/shard_map/all_gather | solution.py:82
  13.8 297.1 %all-gather.29.cloned.1.call-start = ((), (), s32[]{:S(2)}) async-start(), calls=%async_computation.31 | async-start | bytes 4718592 | tf_op jit(solution)/shard_map/all_gather | solution.py:83
  14.5 67.9 %collective-permute-start = (bf16[1,64,512]{2,1,0:T(8,128)(2,1)S(1)}, bf16[1,64,512]{2,1,0:T(8,128)(2,1)S(1)}, u32[]{:S(2)}, u32[]{:S(2)}) collective-permute-start(bf16[1,64,512]{2,1,0:T(8,128)(2,1)S(1)} %get-tuple-element.130), channel_id=1, source_target_pairs={{0,4},{4,0},{8,12},{12,8},{16,20},{20,16},{24,28},{28,24},{1,5},{5... | collective-permute-start | bytes 196616 | tf_op jit(solution)/shard_map/ppermute | solution.py:26
  15.0 141.1 %collective-permute-start.3 = (bf16[1,64,512]{2,1,0:T(8,128)(2,1)}, bf16[1,64,512]{2,1,0:T(8,128)(2,1)}, u32[]{:S(2)}, u32[]{:S(2)}) collective-permute-start(bf16[1,64,512]{2,1,0:T(8,128)(2,1)} %get-tuple-element.129), channel_id=1, source_target_pairs={{0,4},{4,0},{8,12},{12,8},{16,20},{20,16},{24,28},{28,24},{1,5},{5... | collective-permute-start | bytes 196616 | tf_op jit(solution)/shard_map/ppermute | solution.py:26
  33.8 24.7 %copy-start.57 = (s32[394,1]{0,1:T(1,128)}, s32[394,1]{0,1:T(1,128)S(1)}, u32[]{:S(2)}) copy-start(s32[394,1]{0,1:T(1,128)S(1)} %get-tuple-element.139) | copy-start | bytes 4732
  33.8 24.7 %copy-start.60 = (s32[394,1]{0,1:T(1,128)}, s32[394,1]{0,1:T(1,128)S(1)}, u32[]{:S(2)}) copy-start(s32[394,1]{0,1:T(1,128)S(1)} %get-tuple-element.140) | copy-start | bytes 4732
  37.8 55.2 %copy-start.65 = (s32[394,1]{0,1:T(1,128)}, s32[394,1]{0,1:T(1,128)S(1)}, u32[]{:S(2)}) copy-start(s32[394,1]{0,1:T(1,128)S(1)} %get-tuple-element.138) | copy-start | bytes 4732
  37.8 81.4 %copy-start.63 = (s32[394,1]{0,1:T(1,128)}, s32[394,1]{0,1:T(1,128)S(1)}, u32[]{:S(2)}) copy-start(s32[394,1]{0,1:T(1,128)S(1)} %get-tuple-element.137) | copy-start | bytes 4732
  42.7 78.0 %copy-start.91 = (f32[512]{0:T(512)}, f32[512]{0:T(512)S(1)}, u32[]{:S(2)}) copy-start(f32[512]{0:T(512)S(1)} %get-tuple-element.80) | copy-start | bytes 6148
  42.7 99.1 %copy-start.97 = (f32[512]{0:T(512)}, f32[512]{0:T(512)S(1)}, u32[]{:S(2)}) copy-start(f32[512]{0:T(512)S(1)} %get-tuple-element.79) | copy-start | bytes 6148
  82.5 10.5 collective-permute-start.1
  93.0 26.8 %collective-permute-start.2 = (bf16[4,64,512]{2,1,0:T(8,128)(2,1)S(1)}, bf16[4,64,512]{2,1,0:T(8,128)(2,1)S(1)}, u32[]{:S(2)}, u32[]{:S(2)}) collective-permute-start(bf16[4,64,512]{2,1,0:T(8,128)(2,1)S(1)} %bitcast.304), channel_id=1, source_target_pairs={{0,16},{4,20},{8,24},{12,28},{16,0},{20,4},{24,8},{28,12},{1,17},{... | collective-permute-start | bytes 786440 | tf_op jit(solution)/shard_map/ppermute | solution.py:26
  98.1 24.9 %copy-start.8 = (f32[394,512]{1,0:T(8,128)}, f32[394,512]{1,0:T(8,128)S(1)}, u32[]{:S(2)}) copy-start(f32[394,512]{1,0:T(8,128)S(1)} %reshape.353) | copy-start | bytes 2420740
  98.3 24.7 %copy-start.75 = (f32[394]{0:T(512)}, f32[394]{0:T(512)S(1)}, u32[]{:S(2)}) copy-start(f32[394]{0:T(512)S(1)} %rsqrt.40) | copy-start | bytes 4732
  98.4 24.7 %copy-start.77 = (f32[394]{0:T(512)}, f32[394]{0:T(512)S(1)}, u32[]{:S(2)}) copy-start(f32[394]{0:T(512)S(1)} %div.51) | copy-start | bytes 4732
  151.2 28.5 %copy-start.109 = (s32[394]{0:T(512)S(1)}, s32[394]{0:T(512)}, u32[]{:S(2)}) copy-start(s32[394]{0:T(512)} %compare_select_fusion.3) | copy-start | bytes 4732
  151.2 30.8 %all-to-all-start = ((bf16[4,2,147,512]{3,1,2,0:T(2,128)(2,1)}), bf16[4,2,147,512]{3,1,2,0:T(2,128)(2,1)}, u32[]{:S(2)}, u32[]{:S(2)}) async-start(bf16[4,2,147,512]{3,1,2,0:T(2,128)(2,1)} %copy.282), calls=%async_computation | async-start | bytes 2408448 | tf_op jit(solution)/shard_map/all_to_all | solution.py:124
  157.7 22.6 %collective-permute-start.4 = (bf16[2,64,512]{2,1,0:T(8,128)(2,1)}, bf16[2,64,512]{2,1,0:T(8,128)(2,1)}, u32[]{:S(2)}, u32[]{:S(2)}) collective-permute-start(bf16[2,64,512]{2,1,0:T(8,128)(2,1)} %get-tuple-element.126), channel_id=1, source_target_pairs={{0,8},{4,12},{8,0},{12,4},{16,24},{20,28},{24,16},{28,20},{1,9},{5... | collective-permute-start | bytes 393224 | tf_op jit(solution)/shard_map/ppermute | solution.py:26
  181.4 31.8 %collective-permute-start.5 = (bf16[4,64,512]{2,1,0:T(8,128)(2,1)S(1)}, bf16[4,64,512]{2,1,0:T(8,128)(2,1)}, u32[]{:S(2)}, u32[]{:S(2)}) collective-permute-start(bf16[4,64,512]{2,1,0:T(8,128)(2,1)S(1)} %bitcast.306), channel_id=1, source_target_pairs={{0,16},{4,20},{8,24},{12,28},{16,0},{20,4},{24,8},{28,12},{1,17},{... | collective-permute-start | bytes 786440 | tf_op jit(solution)/shard_map/ppermute | solution.py:26
  200.4 20.2 %all-to-all-start.1 = ((bf16[4,2,147,512]{3,1,2,0:T(2,128)(2,1)}), bf16[4,2,147,512]{3,1,2,0:T(2,128)(2,1)}, u32[]{:S(2)}, u32[]{:S(2)}) async-start(bf16[4,2,147,512]{3,1,2,0:T(2,128)(2,1)} %copy.284), calls=%async_computation.1 | async-start | bytes 2408448 | tf_op jit(solution)/shard_map/all_to_all | solution.py:132
  277.5 24.3 %all-to-all-start.2 = ((bf16[4,2,147,512]{3,1,2,0:T(2,128)(2,1)}), bf16[4,2,147,512]{3,1,2,0:T(2,128)(2,1)}, u32[]{:S(2)}, u32[]{:S(2)}) async-start(bf16[4,2,147,512]{3,1,2,0:T(2,128)(2,1)} %copy.300), calls=%async_computation.2 | async-start | bytes 2408448 | tf_op jit(solution)/shard_map/all_to_all | solution.py:124
  319.6 21.0 %all-to-all-start.3 = ((bf16[4,2,147,512]{3,1,2,0:T(2,128)(2,1)}), bf16[4,2,147,512]{3,1,2,0:T(2,128)(2,1)}, u32[]{:S(2)}, u32[]{:S(2)}) async-start(bf16[4,2,147,512]{3,1,2,0:T(2,128)(2,1)} %copy.302), calls=%async_computation.3 | async-start | bytes 2408448 | tf_op jit(solution)/shard_map/all_to_all | solution.py:132
  396.7 18.9 %all-to-all-start.5 = ((bf16[4,2,147,512]{3,1,2,0:T(2,128)(2,1)}), bf16[4,2,147,512]{3,1,2,0:T(2,128)(2,1)}, u32[]{:S(2)}, u32[]{:S(2)}) async-start(bf16[4,2,147,512]{3,1,2,0:T(2,128)(2,1)} %copy.307), calls=%async_computation.5 | async-start | bytes 2408448 | tf_op jit(solution)/shard_map/all_to_all | solution.py:236
  497.3 18.2 %all-to-all-start.7 = ((bf16[4,2,147,512]{3,1,2,0:T(2,128)(2,1)}), bf16[4,2,147,512]{3,1,2,0:T(2,128)(2,1)}, u32[]{:S(2)}, u32[]{:S(2)}) async-start(bf16[4,2,147,512]{3,1,2,0:T(2,128)(2,1)} %copy.323), calls=%async_computation.7 | async-start | bytes 2408448 | tf_op jit(solution)/shard_map/all_to_all | solution.py:236
  501.6 62.5 %reduce-scatter.41.cloned.1.call-start = ((), (), s32[]{:S(2)}) async-start(), calls=%async_computation.35 | async-start | bytes 589824 | tf_op jit(solution)/shard_map/reduce_scatter | solution.py:347
  504.2 63.8 %reduce-scatter.39.cloned.1.call-start = ((), (), s32[]{:S(2)}) async-start(), calls=%async_computation.34 | async-start | bytes 589824 | tf_op jit(solution)/shard_map/reduce_scatter | solution.py:347
  526.6 76.7 %reduce-scatter.37.cloned.1.call-start = ((), (), s32[]{:S(2)}) async-start(), calls=%async_computation.33 | async-start | bytes 1769472 | tf_op jit(solution)/shard_map/reduce_scatter | solution.py:344
  530.8 107.3 %reduce-scatter.35.cloned.1.call-start = ((), (), s32[]{:S(2)}) async-start(), calls=%async_computation.32 | async-start | bytes 1769472 | tf_op jit(solution)/shard_map/reduce_scatter | solution.py:344
  554.8 118.8 %reduce-scatter.45.cloned.1.call-start = ((), (), s32[]{:S(2)}) async-start(), calls=%async_computation.37 | async-start | bytes 147456
  555.9 144.9 %reduce-scatter.53.cloned.1.call-start = ((), (), s32[]{:S(2)}) async-start(), calls=%async_computation.41 | async-start | bytes 147456
  556.8 175.5 %reduce-scatter.49.cloned.1.call-start = ((), (), s32[]{:S(2)}) async-start(), calls=%async_computation.39 | async-start | bytes 147456
  557.7 206.0 %reduce-scatter.43.cloned.1.call-start = ((), (), s32[]{:S(2)}) async-start(), calls=%async_computation.36 | async-start | bytes 147456
  558.7 235.9 %reduce-scatter.51.cloned.1.call-start = ((), (), s32[]{:S(2)}) async-start(), calls=%async_computation.40 | async-start | bytes 147456
  563.1 263.0 %reduce-scatter.47.cloned.1.call-start = ((), (), s32[]{:S(2)}) async-start(), calls=%async_computation.38 | async-start | bytes 147456
  564.0 309.1 %all-reduce.6.cloned.1.call-start = ((), (), s32[]{:S(2)}) async-start(), calls=%async_computation.42 | async-start | bytes 1048576 | tf_op jit(solution)/shard_map/psum | solution.py:337
  638.1 287.0 %reduce-scatter.33.cloned.1.call-start = ((), (), s32[]{:S(2)}) async-start(), calls=%async_computation.25 | async-start | bytes 4718592 | tf_op jit(solution)/shard_map/reduce_scatter | solution.py:364
  646.7 329.1 %reduce-scatter.31.cloned.1.call-start = ((), (), s32[]{:S(2)}) async-start(), calls=%async_computation.24 | async-start | bytes 4718592 | tf_op jit(solution)/shard_map/reduce_scatter | solution.py:364
  656.5 369.9 %reduce-scatter.29.cloned.1.call-start = ((), (), s32[]{:S(2)}) async-start(), calls=%async_computation.23 | async-start | bytes 4718592 | tf_op jit(solution)/shard_map/reduce_scatter | solution.py:361
  665.0 412.2 %reduce-scatter.27.cloned.1.call-start = ((), (), s32[]{:S(2)}) async-start(), calls=%async_computation.22 | async-start | bytes 4718592 | tf_op jit(solution)/shard_map/reduce_scatter | solution.py:361
  673.5 91.0 %copy-start.13 = (f32[394,512]{1,0:T(8,128)S(1)}, f32[394,512]{1,0:T(8,128)}, u32[]{:S(2)}) copy-start(f32[394,512]{1,0:T(8,128)} %copy-done.12) | copy-start | bytes 2420740
  673.5 91.0 %copy-start.49 = (f32[394,512]{1,0:T(8,128)S(1)}, f32[394,512]{1,0:T(8,128)}, u32[]{:S(2)}) copy-start(f32[394,512]{1,0:T(8,128)} %get-tuple-element.172) | copy-start | bytes 2420740
  (127 other events, 528.9 us)
Sparse Core Ops, SparseCore 0:
  10.2 29.3 all-gather.18
  41.2 51.1 all-gather.20
  94.0 50.2 all-gather.22
  146.4 27.8 all-gather.24
  175.7 59.1 all-gather.26
  236.3 46.7 all-gather.28
  504.7 31.5 reduce-scatter.40
  538.5 29.4 reduce-scatter.38
  570.9 32.3 reduce-scatter.36
  605.5 32.5 reduce-scatter.34
  640.9 28.9 reduce-scatter.44
  672.0 28.7 reduce-scatter.52
  703.6 28.6 reduce-scatter.48
  735.0 28.7 reduce-scatter.42
  765.8 28.7 reduce-scatter.50
  797.3 28.7 reduce-scatter.46
  829.1 43.8 all-reduce.5
  875.2 49.8 reduce-scatter.32
  927.4 48.3 reduce-scatter.30
  978.0 48.3 reduce-scatter.28
  1028.7 48.3 reduce-scatter.26
